TPU v7x, 32 devices: a whole 2x2x4 slice. The times are simulated.
32 devices in a mesh: row: 4 (over z), col: 8 (over y, x, core).
Axes of the slice: x: 2, y: 2, z: 4, core: 2. Of those that a mesh axis runs over, the one named last changes fastest.
Arguments:
- pair: bfloat16 [128, 128, 128], P('row', 'col'), may hold values from -6 to 6
- gain_in: float32 [128], replicated, may hold values from 0.1 to 1.9
- w_left_gate: bfloat16 [128, 128], replicated, may hold values from -0.5 to 0.5
- w_left: bfloat16 [128, 128], replicated, may hold values from -0.5 to 0.5
- w_right_gate: bfloat16 [128, 128], replicated, may hold values from -0.5 to 0.5
- w_right: bfloat16 [128, 128], replicated, may hold values from -0.5 to 0.5
- gain_out: float32 [128], replicated, may hold values from 0.1 to 1.9
- w_out_gate: bfloat16 [128, 128], replicated, may hold values from -0.5 to 0.5
- w_out: bfloat16 [128, 128], replicated, may hold values from -0.5 to 0.5
Outputs:
- update: bfloat16 [128, 128, 128], P('row', 'col')
All inputs are finite; a program needn't handle non-finite values.
Results may differ from a plain program's by a relative error of at most 0.0081.
Values may be sent and summed in bfloat16 or wider, within the bound.
A program may use at most 64 MiB of HBM per device.

v0:
```python
import jax
import jax.numpy as jnp
from jax import lax
from jax.sharding import PartitionSpec as P


def spread(value, axis, source):
    kept = jnp.where(lax.axis_index(axis) == source, value, 0).astype(value.dtype)
    return lax.psum(kept, axis)


def layer_norm(values, gain):
    mean = jnp.mean(values, axis=-1, keepdims=True)
    centred = values - mean
    variance = jnp.mean(centred * centred, axis=-1, keepdims=True)
    return centred * lax.rsqrt(variance + 1e-05) * gain


def project(normed, weight):
    return jnp.einsum("ijc,ch->ijh", normed, weight, preferred_element_type=jnp.float32)


def per_device(
    pair, gain_in, w_left_gate, w_left, w_right_gate, w_right, gain_out, w_out_gate, w_out
):
    col_block = pair.shape[1]
    normed = layer_norm(pair.astype(jnp.float32), gain_in).astype(jnp.bfloat16)
    left = (jax.nn.sigmoid(project(normed, w_left_gate)) * project(normed, w_left)).astype(
        jnp.bfloat16
    )
    right = (jax.nn.sigmoid(project(normed, w_right_gate)) * project(normed, w_right)).astype(
        jnp.bfloat16
    )
    panel = lax.all_gather(right, "col", axis=1, tiled=True)
    ratio = lax.axis_size("col") // lax.axis_size("row")
    column = lax.axis_index("col")
    owned = lax.dynamic_slice_in_dim(panel, column % ratio * col_block, col_block, 0)
    right_cols = spread(owned, "row", column // ratio)
    mixed = jnp.einsum(
        "ikh,jkh->ijh",
        lax.all_gather(left, "col", axis=1, tiled=True),
        right_cols,
        preferred_element_type=jnp.float32,
    )
    out_normed = layer_norm(mixed, gain_out).astype(jnp.bfloat16)
    gate = jax.nn.sigmoid(project(normed, w_out_gate))
    return (gate * project(out_normed, w_out)).astype(jnp.bfloat16)


def solution(mesh):
    return jax.shard_map(
        per_device,
        mesh=mesh,
        in_specs=(P("row", "col", None), P(), P(), P(), P(), P(), P(), P(), P()),
        out_specs=P("row", "col", None),
        check_vma=False,
    )
```

profile of v0, /device:TPU:0, one launch (start us, length us, event | category | flops | bytes accessed | tf_op | source)
XLA Modules:
  0.0 118.3 jit_solution(17860925446135129522)
XLA Ops:
  6.6 1.1 convert_reduce_fusion
  7.7 0.1 copy.27
  7.8 0.1 copy.28
  7.8 1.1 fusion.14
  9.0 0.1 copy.29
  9.1 0.1 copy.30
  9.2 1.2 %fusion.5 = f32[32,16,128]{2,1,0:T(8,128)S(1)} fusion(bf16[128,128]{1,0:T(8,128)(2,1)S(1)} %copy-done, bf16[32,16,128]{2,1,0:T(8,128)(2,1)} %param.9, f32[128]{0:T(128)} %param.10, f32[32,16]{1,0:T(8,128)S(1)} %copy.30, f32[32,16]{1,0:T(8,128)S(1)} %copy.28), kind=kOutput, calls=%fused_computation.11 | convolution fusion | flops 17301504 | bytes 430592 | tf_op jit(solution)/shard_map/ijc,ch->ijh/dot_general | solution.py:20
  10.4 1.9 %fusion.9 = bf16[32,16,128]{2,1,0:T(8,128)(2,1)} fusion(f32[32,16,128]{2,1,0:T(8,128)S(1)} %fusion.5, bf16[128,128]{1,0:T(8,128)(2,1)} %param.14, bf16[32,16,128]{2,1,0:T(8,128)(2,1)} %param.9, f32[128]{0:T(128)} %param.10, f32[32,16]{1,0:T(8,128)S(1)} %copy.30, f32[32,16]{1,0:T(8,128)S(1)} %copy.28), kind=kOutput, calls=%fused_computation.16 | convolution fusion | flops 17235968 | bytes 561664 | tf_op jit(solution)/shard_map/ijc,ch->ijh/dot_general | solution.py:20
  12.3 0.0 all-gather.5.cloned.1.call-start
  12.4 1.3 %fusion.2 = f32[32,16,128]{2,1,0:T(8,128)S(1)} fusion(bf16[128,128]{1,0:T(8,128)(2,1)} %param.11, bf16[32,16,128]{2,1,0:T(8,128)(2,1)} %param.9, f32[128]{0:T(128)} %param.10, f32[32,16]{1,0:T(8,128)S(1)} %copy.30, f32[32,16]{1,0:T(8,128)S(1)} %copy.28), kind=kOutput, calls=%fused_computation.7 | convolution fusion | flops 17301504 | bytes 430592 | tf_op jit(solution)/shard_map/ijc,ch->ijh/dot_general | solution.py:20
  13.7 1.9 %fusion.10 = bf16[32,16,128]{2,1,0:T(8,128)(2,1)} fusion(f32[32,16,128]{2,1,0:T(8,128)S(1)} %fusion.2, bf16[128,128]{1,0:T(8,128)(2,1)} %param.12, bf16[32,16,128]{2,1,0:T(8,128)(2,1)} %param.9, f32[128]{0:T(128)} %param.10, f32[32,16]{1,0:T(8,128)S(1)} %copy.30, f32[32,16]{1,0:T(8,128)S(1)} %copy.28), kind=kOutput, calls=%fused_computation.17 | convolution fusion | flops 17235968 | bytes 561664 | tf_op jit(solution)/shard_map/ijc,ch->ijh/dot_general | solution.py:20
  15.6 0.0 all-reduce.2.cloned.1.call-start
  15.7 23.1 %all-gather.3.cloned.1.call-done = bf16[32,128,128]{2,1,0:T(8,128)(2,1)} async-done(((bf16[32,16,128]{2,1,0:T(8,128)(2,1)}), bf16[32,128,128]{2,1,0:T(8,128)(2,1)}) %all-gather.3.cloned.1.call-update) | async-done | bytes 1048592 | tf_op jit(solution)/shard_map/all_gather | solution.py:34
  38.7 1.9 %dynamic-slice_select_fusion = bf16[16,128,128]{2,1,0:T(8,128)(2,1)} fusion(bf16[32,128,128]{2,1,0:T(8,128)(2,1)} %all-gather.3.cloned.1.call-done, s32[]{:T(128)S(6)} %select_n.25, pred[]{:T(512)S(6)} %eq.5), kind=kLoop, calls=%fused_computation.21 | loop fusion | flops 262144 | bytes 1048581 | tf_op jit(solution)/shard_map/jit(_where)/select_n | solution.py:8
  40.6 0.3 fusion.8
  41.0 23.1 %all-gather.5.cloned.1.call-done = bf16[32,128,128]{2,1,0:T(8,128)(2,1)} async-done(((bf16[32,16,128]{2,1,0:T(8,128)(2,1)}), bf16[32,128,128]{2,1,0:T(8,128)(2,1)}) %all-gather.5.cloned.1.call-update) | async-done | bytes 1048592 | tf_op jit(solution)/shard_map/all_gather | solution.py:41
  64.1 8.6 %copy.32 = bf16[32,128,128]{0,1,2:T(8,128)(2,1)} copy(bf16[32,128,128]{2,1,0:T(8,128)(2,1)} %all-gather.5.cloned.1.call-done) | data formatting | bytes 2097152 | tf_op jit(solution)/shard_map/all_gather | solution.py:41
  72.7 32.4 %all-reduce.2.cloned.1.call-done = bf16[16,128,128]{2,1,0:T(8,128)(2,1)} async-done(((bf16[16,128,128]{2,1,0:T(8,128)(2,1)}), bf16[16,128,128]{2,1,0:T(8,128)(2,1)}) %all-reduce.2.cloned.1.call-update) | async-done | bytes 524304 | tf_op jit(solution)/shard_map/psum | solution.py:9
  105.1 1.5 %copy.31 = bf16[16,128,128]{1,0,2:T(8,128)(2,1)S(1)} copy(bf16[16,128,128]{2,1,0:T(8,128)(2,1)} %all-reduce.2.cloned.1.call-done) | data formatting | bytes 1048576 | tf_op jit(solution)/shard_map/psum | solution.py:9
  106.6 3.4 %fusion.28 = (f32[32,16]{0,1:T(8,128)S(1)}, f32[32,16,128]{0,1,2:T(8,128)S(1)}) fusion(bf16[16,128,128]{1,0,2:T(8,128)(2,1)S(1)} %copy.31, bf16[32,128,128]{0,1,2:T(8,128)(2,1)} %copy.32), kind=kOutput, calls=%fused_computation.39 | convolution fusion | flops 16842240 | bytes 1837056 | tf_op jit(solution)/shard_map/ikh,jkh->ijh/dot_general | solution.py:39
  110.0 0.2 multiply_reduce_fusion
  110.2 0.2 multiply_convert_fusion
  110.4 0.5 copy.33
  110.9 0.8 fusion.11
  (20 shorter events, 0.1 us)
Async XLA Ops:
  6.5 2.6 %copy-start = (bf16[128,128]{1,0:T(8,128)(2,1)S(1)}, bf16[128,128]{1,0:T(8,128)(2,1)}, u32[]{:S(2)}) copy-start(bf16[128,128]{1,0:T(8,128)(2,1)} %param.13) | copy-start | bytes 98308
  6.5 34.1 %copy-start.1 = (bf16[32,16,128]{2,1,0:T(8,128)(2,1)S(1)}, bf16[32,16,128]{2,1,0:T(8,128)(2,1)}, u32[]{:S(2)}) copy-start(bf16[32,16,128]{2,1,0:T(8,128)(2,1)} %param.9) | copy-start | bytes 393220
  6.5 34.1 %copy-start.3 = (f32[128]{0:T(128)S(1)}, f32[128]{0:T(128)}, u32[]{:S(2)}) copy-start(f32[128]{0:T(128)} %param.10) | copy-start | bytes 1540
  6.5 34.1 %copy-start.5 = (bf16[128,128]{1,0:T(8,128)(2,1)S(1)}, bf16[128,128]{1,0:T(8,128)(2,1)}, u32[]{:S(2)}) copy-start(bf16[128,128]{1,0:T(8,128)(2,1)} %param.16) | copy-start | bytes 98308
  6.5 32.2 %all-gather.3.cloned.1.call-start = ((), (), s32[]{:S(2)}) async-start(), calls=%async_computation | async-start | bytes 1179648 | tf_op jit(solution)/shard_map/all_gather | solution.py:34
  12.3 51.7 %all-gather.5.cloned.1.call-start = ((), (), s32[]{:S(2)}) async-start(), calls=%async_computation.2 | async-start | bytes 1179648 | tf_op jit(solution)/shard_map/all_gather | solution.py:41
  15.6 89.5 %all-reduce.2.cloned.1.call-start = ((), (), s32[]{:S(2)}) async-start(), calls=%async_computation.1 | async-start | bytes 1048576 | tf_op jit(solution)/shard_map/psum | solution.py:9
  72.7 37.5 %copy-start.4 = (f32[128]{0:T(128)S(1)}, f32[128]{0:T(128)}, u32[]{:S(2)}) copy-start(f32[128]{0:T(128)} %param.15) | copy-start | bytes 1540
  106.6 4.4 %copy-start.2 = (bf16[128,128]{1,0:T(8,128)(2,1)S(1)}, bf16[128,128]{1,0:T(8,128)(2,1)}, u32[]{:S(2)}) copy-start(bf16[128,128]{1,0:T(8,128)(2,1)} %param.17) | copy-start | bytes 98308
Sparse Core Ops, SparseCore 0:
  12.5 26.1 all-gather.2
  40.6 23.4 all-gather.4
  66.4 38.6 all-reduce.1
where the time goes:
time: 119 us; the launch traced here: 118 us
  waiting for transfers between devices  78.6 us (66%)
  between operations  13.3 us (11%)
  local copies, waits for them, and re-layouts  10.9 us (9%)
  matrix products  10.9 us (9%)
  other arithmetic  4.59 us (4%)
    psum x1, waiting for transfers between devices, spread(): return lax.psum(kept, axis)  32.4 us
    all_gather x1, waiting for transfers between devices, per_device(): lax.all_gather(left, 'col', axis=1, tiled=True)  23.1 us
    all_gather x1, waiting for transfers between devices, per_device(): panel = lax.all_gather(right, 'col', axis=1, tiled=True)  23.1 us
    all_gather x1, local copies, waits for them, and re-layouts, per_device(): lax.all_gather(left, 'col', axis=1, tiled=True)  8.61 us
    dot_general x6, matrix products, project(): jnp.einsum('ijc,ch->ijh', normed, weight, preferred_element_type=jnp.floa...  7.46 us
    dot_general x1, matrix products, per_device(): jnp.einsum('ikh,jkh->ijh', lax.all_gather(left, 'col', axis=1, tiled=True...  3.39 us
  transfers between devices with their start and end apart: 3, of which 3 were waited for; matrix products, arithmetic and copies ran while one was open for 12% of the time, Pallas kernels for 0%

commit v1 on v0

--- a/solution.py
+++ b/solution.py
@@ -2,6 +2,28 @@
 import jax.numpy as jnp
 from jax import lax
 from jax.sharding import PartitionSpec as P
+
+
+def laid_out(blocks, dim):
+    dims = list(blocks.shape[1:])
+    dims[dim] *= blocks.shape[0]
+    return jnp.moveaxis(blocks, 0, dim).reshape(dims)
+
+
+def ring_gather(x, axis, dim):
+    size = lax.axis_size(axis)
+    pairs = [(i, (i + 1) % size) for i in range(size)]
+    back = [(b, a) for a, b in pairs]
+    lower, upper = ([], [])
+    for step in range(size - 1):
+        if step % 2 == 0:
+            lower.append(lax.ppermute(lower[-1] if lower else x, axis, pairs))
+        else:
+            upper.append(lax.ppermute(upper[-1] if upper else x, axis, back))
+    blocks = jnp.stack([*lower[::-1], x, *upper])
+    shift = lax.axis_index(axis) - len(lower)
+    blocks = blocks[(jnp.arange(size) - shift) % size]
+    return laid_out(blocks, dim)
 
 
 def spread(value, axis, source):
@@ -37,10 +59,7 @@
     owned = lax.dynamic_slice_in_dim(panel, column % ratio * col_block, col_block, 0)
     right_cols = spread(owned, "row", column // ratio)
     mixed = jnp.einsum(
-        "ikh,jkh->ijh",
-        lax.all_gather(left, "col", axis=1, tiled=True),
-        right_cols,
-        preferred_element_type=jnp.float32,
+        "ikh,jkh->ijh", ring_gather(left, "col", 1), right_cols, preferred_element_type=jnp.float32
     )
     out_normed = layer_norm(mixed, gain_out).astype(jnp.bfloat16)
     gate = jax.nn.sigmoid(project(normed, w_out_gate))

time: 119 us -> 93 us (0.78)
  waiting for transfers between devices: 78.6 us -> 55.7 us
  starting transfers between devices: 0.12 us -> 8.57 us
  matrix products: 10.9 us -> 4.47 us
  local copies, waits for them, and re-layouts: 10.9 us -> 6.5 us
    all_gather x1 -> x0, waiting for transfers between devices: 23.1 us -> none  [per_device(): lax.all_gather(left, 'col', axis=1, tiled=True)]
    all_gather x1, waiting for transfers between devices: 23.1 us -> 4.05 us  [per_device(): panel = lax.all_gather(right, 'col', axis=1, tiled=True)]
    ppermute x0 -> x7, waiting for transfers between devices: none -> 14 us  [the longest x4 14 us: ring_gather(): lower.append(lax.ppermute(lower[-1] if lower else x, axis, pairs))]
    all_gather x1 -> x0, local copies, waits for them, and re-layouts: 8.61 us -> none  [per_device(): lax.all_gather(left, 'col', axis=1, tiled=True)]
    ppermute x0 -> x7, starting transfers between devices: none -> 8.53 us  [the longest x3 7.98 us: ring_gather(): upper.append(lax.ppermute(upper[-1] if upper else x, axis, back))]
    psum x1, waiting for transfers between devices: 32.4 us -> 37.6 us  [spread(): return lax.psum(kept, axis)]
    dot_general x6, matrix products: 7.46 us -> 3.81 us  [project(): jnp.einsum('ijc,ch->ijh', normed, weight, preferred_element_type=jnp.floa...]
    dot_general x1, matrix products: 3.39 us -> 0.66 us  [per_device(): jnp.einsum('ikh,jkh->ijh', ring_gather(left, 'col', 1), right_cols, prefe...]
  transfers between devices with their start and end apart: 3 -> 9, of which waited for: 3 -> 6; matrix products, arithmetic and copies ran while one was open for 12% -> 7% of each run, Pallas kernels for 0% -> 0%
where the time goes in v1:
time: 93 us; the launch traced here: 92.6 us
  waiting for transfers between devices  55.7 us (60%)
  between operations  13.7 us (15%)
  starting transfers between devices  8.57 us (9%)
  local copies, waits for them, and re-layouts  6.5 us (7%)
  matrix products  4.47 us (5%)
  other arithmetic  3.71 us (4%)
    psum x1, waiting for transfers between devices, spread(): return lax.psum(kept, axis)  37.6 us
    ppermute x4, waiting for transfers between devices, ring_gather(): lower.append(lax.ppermute(lower[-1] if lower else x, axis, pairs))  14 us
    ppermute x3, starting transfers between devices, ring_gather(): upper.append(lax.ppermute(upper[-1] if upper else x, axis, back))  7.98 us
    all_gather x1, waiting for transfers between devices, per_device(): panel = lax.all_gather(right, 'col', axis=1, tiled=True)  4.05 us
    dot_general x6, matrix products, project(): jnp.einsum('ijc,ch->ijh', normed, weight, preferred_element_type=jnp.floa...  3.81 us
    unnamed x27, local copies, waits for them, and re-layouts  2.22 us
    select_n x1, other arithmetic, spread(): jnp.where(lax.axis_index(axis) == source, value, 0).astype(value.dtype)  1.9 us
  transfers between devices with their start and end apart: 9, of which 6 were waited for; matrix products, arithmetic and copies ran while one was open for 7% of the time, Pallas kernels for 0%

profile of v1, /device:TPU:0, one launch (start us, length us, event | category | flops | bytes accessed | tf_op | source)
XLA Modules:
  0.0 92.6 jit_solution(1647002349421057554)
XLA Ops:
  6.5 1.1 %convert_reduce_fusion = f32[32,16]{1,0:T(8,128)S(1)} fusion(bf16[32,16,128]{2,1,0:T(8,128)(2,1)} %param.9), kind=kLoop, calls=%fused_computation.24 | loop fusion | flops 130560 | bytes 133120 | tf_op jit(solution)/shard_map/reduce_sum | solution.py:35
  8.2 0.6 copy-done.6
  9.2 0.4 copy-done.4
  9.9 0.5 collective-permute-start
  10.8 1.0 %fusion.9 = bf16[32,16,128]{2,1,0:T(8,128)(2,1)} fusion(f32[32,16,128]{2,1,0:T(8,128)S(1)} %fusion.5, bf16[128,128]{1,0:T(8,128)(2,1)S(1)} %copy-done.5, bf16[32,16,128]{2,1,0:T(8,128)(2,1)S(1)} %copy-done.1, f32[128]{0:T(128)S(1)} %copy-done.6, f32[32,16]{1,0:T(8,128)S(1)} %copy.37, f32[32,16]{1,0:T(8,128)S(1)} %copy.35), kind=kOutput, calls=%fused_computation.17 | convolution fusion | flops 17235968 | bytes 561664 | tf_op jit(solution)/shard_map/ijc,ch->ijh/dot_general | solution.py:42
  11.9 4.1 %collective-permute-done = bf16[32,16,128]{2,1,0:T(8,128)(2,1)S(1)} collective-permute-done((bf16[32,16,128]{2,1,0:T(8,128)(2,1)S(1)}, bf16[32,16,128]{2,1,0:T(8,128)(2,1)S(1)}, u32[]{:S(2)}, u32[]{:S(2)}) %collective-permute-start) | collective-permute-done | bytes 131104 | tf_op jit(solution)/shard_map/ppermute | solution.py:20
  16.0 2.6 %collective-permute-start.4 = (bf16[32,16,128]{2,1,0:T(8,128)(2,1)S(1)}, bf16[32,16,128]{2,1,0:T(8,128)(2,1)S(1)}, u32[]{:S(2)}, u32[]{:S(2)}) collective-permute-start(bf16[32,16,128]{2,1,0:T(8,128)(2,1)S(1)} %fusion.10), channel_id=1, source_target_pairs={{1,0},{2,1},{3,2},{4,3},{5,4},{6,5},{7,6},{0,7},{9,8},{10,9},{11,1... | collective-permute-start | bytes 393224 | tf_op jit(solution)/shard_map/ppermute | solution.py:22
  18.6 2.6 %collective-permute-done.1 = bf16[32,16,128]{2,1,0:T(8,128)(2,1)S(1)} collective-permute-done((bf16[32,16,128]{2,1,0:T(8,128)(2,1)S(1)}, bf16[32,16,128]{2,1,0:T(8,128)(2,1)S(1)}, u32[]{:S(2)}, u32[]{:S(2)}) %collective-permute-start.1) | collective-permute-done | bytes 131104 | tf_op jit(solution)/shard_map/ppermute | solution.py:20
  21.3 1.0 %fusion.8 = f32[32,16,128]{2,1,0:T(8,128)} fusion(bf16[128,128]{1,0:T(8,128)(2,1)S(1)} %copy-done.9, bf16[32,16,128]{2,1,0:T(8,128)(2,1)S(1)} %copy-done.1, f32[128]{0:T(128)S(1)} %copy-done.6, f32[32,16]{1,0:T(8,128)S(1)} %copy.37, f32[32,16]{1,0:T(8,128)S(1)} %copy.35), kind=kOutput, calls=%fused_computation.16 | convolution fusion | flops 17301504 | bytes 430592 | tf_op jit(solution)/shard_map/ijc,ch->ijh/dot_general | solution.py:42
  22.3 2.6 %collective-permute-start.5 = (bf16[32,16,128]{2,1,0:T(8,128)(2,1)S(1)}, bf16[32,16,128]{2,1,0:T(8,128)(2,1)S(1)}, u32[]{:S(2)}, u32[]{:S(2)}) collective-permute-start(bf16[32,16,128]{2,1,0:T(8,128)(2,1)S(1)} %collective-permute-done.4), channel_id=1, source_target_pairs={{1,0},{2,1},{3,2},{4,3},{5,4},{6,5},{7,6},{0,7},{9,8},{10,9},{11,1... | collective-permute-start | bytes 393224 | tf_op jit(solution)/shard_map/ppermute | solution.py:22
  24.9 3.6 %collective-permute-done.2 = bf16[32,16,128]{2,1,0:T(8,128)(2,1)S(1)} collective-permute-done((bf16[32,16,128]{2,1,0:T(8,128)(2,1)S(1)}, bf16[32,16,128]{2,1,0:T(8,128)(2,1)S(1)}, u32[]{:S(2)}, u32[]{:S(2)}) %collective-permute-start.2) | collective-permute-done | bytes 131104 | tf_op jit(solution)/shard_map/ppermute | solution.py:20
  28.6 2.7 %collective-permute-start.6 = (bf16[32,16,128]{2,1,0:T(8,128)(2,1)S(1)}, bf16[32,16,128]{2,1,0:T(8,128)(2,1)S(1)}, u32[]{:S(2)}, u32[]{:S(2)}) collective-permute-start(bf16[32,16,128]{2,1,0:T(8,128)(2,1)S(1)} %collective-permute-done.5), channel_id=1, source_target_pairs={{1,0},{2,1},{3,2},{4,3},{5,4},{6,5},{7,6},{0,7},{9,8},{10,9},{11,1... | collective-permute-start | bytes 393224 | tf_op jit(solution)/shard_map/ppermute | solution.py:22
  31.3 3.7 %collective-permute-done.3 = bf16[32,16,128]{2,1,0:T(8,128)(2,1)S(1)} collective-permute-done((bf16[32,16,128]{2,1,0:T(8,128)(2,1)S(1)}, bf16[32,16,128]{2,1,0:T(8,128)(2,1)S(1)}, u32[]{:S(2)}, u32[]{:S(2)}) %collective-permute-start.3) | collective-permute-done | bytes 131104 | tf_op jit(solution)/shard_map/ppermute | solution.py:20
  35.1 4.1 %all-gather.2.cloned.1.call-done = bf16[32,128,128]{2,1,0:T(8,128)(2,1)} async-done(((bf16[32,16,128]{2,1,0:T(8,128)(2,1)}), bf16[32,128,128]{2,1,0:T(8,128)(2,1)}) %all-gather.2.cloned.1.call-update) | async-done | bytes 1048592 | tf_op jit(solution)/shard_map/all_gather | solution.py:56
  39.1 1.9 %dynamic-slice_select_fusion = bf16[16,128,128]{2,1,0:T(8,128)(2,1)} fusion(bf16[32,128,128]{2,1,0:T(8,128)(2,1)} %all-gather.2.cloned.1.call-done, s32[]{:T(128)S(6)} %select_n.48, pred[]{:T(512)S(6)} %eq.7), kind=kLoop, calls=%fused_computation.22 | loop fusion | flops 262144 | bytes 1048581 | tf_op jit(solution)/shard_map/jit(_where)/select_n | solution.py:30
  41.2 0.7 gather_fusion
  42.2 1.0 %copy.40 = bf16[32,128,128]{1,0,2:T(8,128)(2,1)S(1)} copy(bf16[32,128,128]{2,1,0:T(8,128)(2,1)S(1)} %bitcast.44) | data formatting | bytes 2097152 | tf_op jit(solution)/shard_map/reshape | solution.py:10
  43.2 37.6 %all-reduce.2.cloned.1.call-done = bf16[16,128,128]{2,1,0:T(8,128)(2,1)} async-done(((bf16[16,128,128]{2,1,0:T(8,128)(2,1)}), bf16[16,128,128]{2,1,0:T(8,128)(2,1)}) %all-reduce.2.cloned.1.call-update) | async-done | bytes 524304 | tf_op jit(solution)/shard_map/psum | solution.py:31
  80.8 1.5 %copy.39 = bf16[16,128,128]{1,0,2:T(8,128)(2,1)S(1)} copy(bf16[16,128,128]{2,1,0:T(8,128)(2,1)} %all-reduce.2.cloned.1.call-done) | data formatting | bytes 1048576 | tf_op jit(solution)/shard_map/psum | solution.py:31
  82.3 0.7 fusion.30
  83.2 0.6 copy-done.7
  84.0 0.5 copy.41
  84.5 0.4 copy-done.2
  85.0 0.8 fusion.11
  (51 shorter events, 2.5 us)
Async XLA Ops:
  6.5 1.7 %copy-start = (bf16[128,128]{1,0:T(8,128)(2,1)S(1)}, bf16[128,128]{1,0:T(8,128)(2,1)}, u32[]{:S(2)}) copy-start(bf16[128,128]{1,0:T(8,128)(2,1)} %param.11) | copy-start | bytes 98308
  6.5 1.3 %copy-start.1 = (bf16[32,16,128]{2,1,0:T(8,128)(2,1)S(1)}, bf16[32,16,128]{2,1,0:T(8,128)(2,1)}, u32[]{:S(2)}) copy-start(bf16[32,16,128]{2,1,0:T(8,128)(2,1)} %param.9) | copy-start | bytes 393220
  6.5 32.6 %all-gather.2.cloned.1.call-start = ((), (), s32[]{:S(2)}) async-start(), calls=%async_computation | async-start | bytes 1179648 | tf_op jit(solution)/shard_map/all_gather | solution.py:56
  8.1 0.7 copy-start.6
  8.8 0.8 copy-start.4
  9.6 0.9 copy-start.8
  9.9 0.9 copy-start.5
  9.9 6.1 %collective-permute-start = (bf16[32,16,128]{2,1,0:T(8,128)(2,1)S(1)}, bf16[32,16,128]{2,1,0:T(8,128)(2,1)S(1)}, u32[]{:S(2)}, u32[]{:S(2)}) collective-permute-start(bf16[32,16,128]{2,1,0:T(8,128)(2,1)S(1)} %fusion.10), channel_id=1, source_target_pairs={{0,1},{1,2},{2,3},{3,4},{4,5},{5,6},{6,7},{7,0},{8,9},{9,10},{10,1... | collective-permute-start | bytes 393224 | tf_op jit(solution)/shard_map/ppermute | solution.py:20
  11.8 9.5 %copy-start.9 = (bf16[128,128]{1,0:T(8,128)(2,1)S(1)}, bf16[128,128]{1,0:T(8,128)(2,1)}, u32[]{:S(2)}) copy-start(bf16[128,128]{1,0:T(8,128)(2,1)} %param.16) | copy-start | bytes 98308
  11.8 69.0 %all-reduce.2.cloned.1.call-start = ((), (), s32[]{:S(2)}) async-start(), calls=%async_computation.1 | async-start | bytes 1048576 | tf_op jit(solution)/shard_map/psum | solution.py:31
  16.0 5.3 %collective-permute-start.1 = (bf16[32,16,128]{2,1,0:T(8,128)(2,1)S(1)}, bf16[32,16,128]{2,1,0:T(8,128)(2,1)S(1)}, u32[]{:S(2)}, u32[]{:S(2)}) collective-permute-start(bf16[32,16,128]{2,1,0:T(8,128)(2,1)S(1)} %collective-permute-done), channel_id=1, source_target_pairs={{0,1},{1,2},{2,3},{3,4},{4,5},{5,6},{6,7},{7,0},{8,9},{9,10},{10,1... | collective-permute-start | bytes 393224 | tf_op jit(solution)/shard_map/ppermute | solution.py:20
  16.0 6.3 %collective-permute-start.4 = (bf16[32,16,128]{2,1,0:T(8,128)(2,1)S(1)}, bf16[32,16,128]{2,1,0:T(8,128)(2,1)S(1)}, u32[]{:S(2)}, u32[]{:S(2)}) collective-permute-start(bf16[32,16,128]{2,1,0:T(8,128)(2,1)S(1)} %fusion.10), channel_id=1, source_target_pairs={{1,0},{2,1},{3,2},{4,3},{5,4},{6,5},{7,6},{0,7},{9,8},{10,9},{11,1... | collective-permute-start | bytes 393224 | tf_op jit(solution)/shard_map/ppermute | solution.py:22
  21.3 7.3 %collective-permute-start.2 = (bf16[32,16,128]{2,1,0:T(8,128)(2,1)S(1)}, bf16[32,16,128]{2,1,0:T(8,128)(2,1)S(1)}, u32[]{:S(2)}, u32[]{:S(2)}) collective-permute-start(bf16[32,16,128]{2,1,0:T(8,128)(2,1)S(1)} %collective-permute-done.1), channel_id=1, source_target_pairs={{0,1},{1,2},{2,3},{3,4},{4,5},{5,6},{6,7},{7,0},{8,9},{9,10},{10,1... | collective-permute-start | bytes 393224 | tf_op jit(solution)/shard_map/ppermute | solution.py:20
  22.3 6.3 %collective-permute-start.5 = (bf16[32,16,128]{2,1,0:T(8,128)(2,1)S(1)}, bf16[32,16,128]{2,1,0:T(8,128)(2,1)S(1)}, u32[]{:S(2)}, u32[]{:S(2)}) collective-permute-start(bf16[32,16,128]{2,1,0:T(8,128)(2,1)S(1)} %collective-permute-done.4), channel_id=1, source_target_pairs={{1,0},{2,1},{3,2},{4,3},{5,4},{6,5},{7,6},{0,7},{9,8},{10,9},{11,1... | collective-permute-start | bytes 393224 | tf_op jit(solution)/shard_map/ppermute | solution.py:22
  28.5 6.5 %collective-permute-start.3 = (bf16[32,16,128]{2,1,0:T(8,128)(2,1)S(1)}, bf16[32,16,128]{2,1,0:T(8,128)(2,1)S(1)}, u32[]{:S(2)}, u32[]{:S(2)}) collective-permute-start(bf16[32,16,128]{2,1,0:T(8,128)(2,1)S(1)} %collective-permute-done.2), channel_id=1, source_target_pairs={{0,1},{1,2},{2,3},{3,4},{4,5},{5,6},{6,7},{7,0},{8,9},{9,10},{10,1... | collective-permute-start | bytes 393224 | tf_op jit(solution)/shard_map/ppermute | solution.py:20
  28.6 12.5 %collective-permute-start.6 = (bf16[32,16,128]{2,1,0:T(8,128)(2,1)S(1)}, bf16[32,16,128]{2,1,0:T(8,128)(2,1)S(1)}, u32[]{:S(2)}, u32[]{:S(2)}) collective-permute-start(bf16[32,16,128]{2,1,0:T(8,128)(2,1)S(1)} %collective-permute-done.5), channel_id=1, source_target_pairs={{1,0},{2,1},{3,2},{4,3},{5,4},{6,5},{7,6},{0,7},{9,8},{10,9},{11,1... | collective-permute-start | bytes 393224 | tf_op jit(solution)/shard_map/ppermute | solution.py:22
  83.1 0.7 copy-start.7
  84.0 1.0 %copy-start.2 = (f32[32,16,128]{2,1,0:T(8,128)S(1)}, f32[32,16,128]{2,1,0:T(8,128)}, u32[]{:S(2)}) copy-start(f32[32,16,128]{2,1,0:T(8,128)} %fusion.8) | copy-start | bytes 786436
  84.0 0.9 %copy-start.3 = (bf16[128,128]{1,0:T(8,128)(2,1)S(1)}, bf16[128,128]{1,0:T(8,128)(2,1)}, u32[]{:S(2)}) copy-start(bf16[128,128]{1,0:T(8,128)(2,1)} %param.17) | copy-start | bytes 98308
Sparse Core Ops, SparseCore 0:
  11.9 27.1 all-gather.1
  41.5 39.2 all-reduce.1
